TPU v7x, 32 devices: a whole 2x2x4 slice. The times are simulated.
32 devices in a mesh: tx: 4 (over z), cell: 8 (over y, x, core).
Axes of the slice: x: 2, y: 2, z: 4, core: 2. Of those that a mesh axis runs over, the one named last changes fastest.
Arguments:
- currents: bfloat16 [2, 2, 8192, 4096], P(None, None, 'cell', 'tx'), may hold values from -6 to 6
- green: bfloat16 [2, 2, 64, 8192], P(None, None, 'tx', 'cell'), may hold values from -0.0625 to 0.0625
- angular_freq: float32 [2], replicated, may hold values from 0.5 to 3
- gate_time: float32 [64], replicated, may hold values from 0.1 to 3
Outputs:
- gated: float32 [64, 64, 4096], P(None, 'cell', 'tx')
All inputs are finite; a program needn't handle non-finite values.
Results may differ from a plain program's by a relative error of at most 0.0003.
Values may be sent and summed in bfloat16 or wider, within the bound.
No kernel may reach another device: no remote copies, remote signals or barrier semaphores. Data moves between devices by JAX's collectives and lax.ppermute only.
A program may use at most 128 MiB of HBM per device.

v0:
```python
import jax
import jax.numpy as jnp
from jax import lax
from jax.sharding import PartitionSpec as P


def complex_rows(green_block, currents):
    real_list = []
    imag_list = []
    for which_freq in range(currents.shape[1]):
        green_real = green_block[0, which_freq]
        green_imag = green_block[1, which_freq]
        curr_real = currents[0, which_freq]
        curr_imag = currents[1, which_freq]
        real_list.append(
            jnp.dot(green_real, curr_real, preferred_element_type=jnp.float32)
            - jnp.dot(green_imag, curr_imag, preferred_element_type=jnp.float32)
        )
        imag_list.append(
            jnp.dot(green_real, curr_imag, preferred_element_type=jnp.float32)
            + jnp.dot(green_imag, curr_real, preferred_element_type=jnp.float32)
        )
    return jnp.stack([jnp.stack(real_list), jnp.stack(imag_list)])


def per_device(currents, green, angular_freq, gate_time):
    gate_phase = gate_time[:, None] * angular_freq[None, :]
    cosine_weight = jnp.cos(gate_phase)
    sine_weight = jnp.sin(gate_phase)
    all_green = lax.all_gather(green, "tx", axis=2, tiled=True)
    receiver_portions = lax.psum_scatter(
        jnp.moveaxis(complex_rows(all_green, currents), 2, 0),
        "cell",
        scatter_dimension=0,
        tiled=True,
    )
    gated = jnp.einsum(
        "qc,ncm->qnm", cosine_weight, receiver_portions[:, 0], precision=lax.Precision.HIGHEST
    )
    gated = gated - jnp.einsum(
        "qc,ncm->qnm", sine_weight, receiver_portions[:, 1], precision=lax.Precision.HIGHEST
    )
    return gated


def solution(mesh):
    return jax.shard_map(
        per_device,
        mesh=mesh,
        in_specs=(P(None, None, "cell", "tx"), P(None, None, "tx", "cell"), P(), P()),
        out_specs=P(None, "cell", "tx"),
        check_vma=False,
    )
```

profile of v0, /device:TPU:0, one launch (start us, length us, event | category | flops | bytes accessed | tf_op | source)
XLA Modules:
  0.0 88.4 jit_solution(19578362142502962)
XLA Ops:
  6.5 0.0 reduce-scatter.2.cloned.1.call-start
  6.5 17.6 %all_gather.3 = bf16[2,2,64,1024]{3,2,1,0:T(8,128)(2,1)S(1)} all-gather(bf16[2,2,16,1024]{3,2,1,0:T(8,128)(2,1)} %param.5), channel_id=1, replica_groups=mesh['tx'=4,'cell'=8] {'tx'}, dimensions={2}, use_global_device_ids=true | all-gather | bytes 655360 | tf_op jit(solution)/shard_map/all_gather | solution.py:30
  24.1 0.0 copy-start
  24.1 2.2 %fusion = f32[64,1024]{1,0:T(8,128)S(1)} fusion(bf16[2,2,1024,1024]{3,2,1,0:T(8,128)(2,1)} %param.4, bf16[2,2,64,1024]{3,2,1,0:T(8,128)(2,1)S(1)} %all_gather.3), kind=kOutput, calls=%fused_computation | convolution fusion | flops 134217728 | bytes 2490368 | tf_op jit(solution)/shard_map/dot_general | solution.py:20
  26.3 2.5 %fusion.8 = f32[64,1024]{1,0:T(8,128)S(1)} fusion(bf16[2,2,1024,1024]{3,2,1,0:T(8,128)(2,1)} %param.4, bf16[2,2,64,1024]{3,2,1,0:T(8,128)(2,1)S(1)} %all_gather.3), kind=kOutput, calls=%fused_computation.8 | convolution fusion | flops 134217728 | bytes 2490368 | tf_op jit(solution)/shard_map/dot_general | solution.py:20
  28.8 2.1 %fusion.2 = f32[64,1024]{1,0:T(8,128)S(1)} fusion(bf16[2,2,1024,1024]{3,2,1,0:T(8,128)(2,1)} %param.4, bf16[2,2,64,1024]{3,2,1,0:T(8,128)(2,1)S(1)} %all_gather.3), kind=kOutput, calls=%fused_computation.2 | convolution fusion | flops 134217728 | bytes 2490368 | tf_op jit(solution)/shard_map/dot_general | solution.py:17
  30.9 2.1 %fusion.10 = f32[64,1024]{1,0:T(8,128)S(1)} fusion(bf16[2,2,1024,1024]{3,2,1,0:T(8,128)(2,1)} %param.4, bf16[2,2,64,1024]{3,2,1,0:T(8,128)(2,1)S(1)} %all_gather.3), kind=kOutput, calls=%fused_computation.10 | convolution fusion | flops 134217728 | bytes 2490368 | tf_op jit(solution)/shard_map/dot_general | solution.py:17
  33.0 0.0 copy-done
  33.0 0.5 fusion.45
  33.5 0.5 fusion.33
  34.0 0.5 fusion.39
  34.5 0.5 fusion.27
  35.0 0.1 maximum_bitcast_fusion.1
  35.0 0.0 copy-start.1
  35.0 0.0 copy-start.2
  35.1 1.1 %maximum_bitcast_fusion = f32[64,2,2,1024]{3,0,2,1:T(8,128)} fusion(f32[1,2,64,1024]{3,2,1,0:T(8,128)S(1)} %get-tuple-element.8, f32[1,2,64,1024]{3,2,1,0:T(8,128)S(1)} %get-tuple-element.7), kind=kLoop, calls=%fused_computation.33 | loop fusion | flops 262144 | bytes 2097152 | tf_op jit(solution)/shard_map/transpose | solution.py:32
  36.1 0.0 reduce-scatter.2.cloned.1.call-update
  36.2 38.0 %reduce-scatter.2.cloned.1.call-done = f32[8,2,2,1024]{3,0,2,1:T(8,128)} async-done(((f32[64,2,2,1024]{3,0,2,1:T(8,128)}), f32[8,2,2,1024]{3,0,2,1:T(8,128)}) %reduce-scatter.2.cloned.1.call-update) | async-done | bytes 131088 | tf_op jit(solution)/shard_map/reduce_scatter | solution.py:31
  74.1 0.9 slice_bitcast_fusion.12
  75.0 0.0 copy-done.1
  75.0 0.0 copy-done.2
  75.0 2.0 %fusion.49 = f32[64,8,1024]{2,0,1:T(8,128)S(1)} fusion(f32[8,2,1024]{2,0,1:T(8,128)S(1)} %get-tuple-element.6, f32[64]{0:T(128)S(1)} %copy-done.1, f32[2]{0:T(128)S(1)} %copy-done.2), kind=kOutput, calls=%fused_computation.43 | convolution fusion | flops 12583040 | bytes 2162952 | tf_op jit(solution)/shard_map/qc,ncm->qnm/dot_general | solution.py:37
  77.0 2.0 %convolution_subtract_fusion = f32[64,8,1024]{2,0,1:T(8,128)S(1)} fusion(f32[64,8,1024]{2,0,1:T(8,128)S(1)} %fusion.49, f32[8,2,1024]{2,0,1:T(8,128)S(1)} %get-tuple-element.5, f32[64]{0:T(128)S(1)} %copy-done.1, f32[2]{0:T(128)S(1)} %copy-done.2), kind=kOutput, calls=%fused_computation.24 | convolution fusion | flops 13107328 | bytes 4260104 | tf_op jit(solution)/shard_map/qc,ncm->qnm/dot_general | solution.py:40
  79.0 2.5 %copy.7 = f32[64,8,1024]{2,1,0:T(8,128)} copy(f32[64,8,1024]{2,0,1:T(8,128)S(1)} %convolution_subtract_fusion) | data formatting | bytes 4194304 | tf_op jit(solution)/shard_map/sub | solution.py:40
Async XLA Ops:
  6.5 67.6 %reduce-scatter.2.cloned.1.call-start = ((), (), s32[]{:S(2)}) async-start(), calls=%async_computation.1 | async-start | bytes 1179648 | tf_op jit(solution)/shard_map/reduce_scatter | solution.py:31
  24.1 8.9 %copy-start = (bf16[2,2,1024,1024]{3,2,1,0:T(8,128)(2,1)S(1)}, bf16[2,2,1024,1024]{3,2,1,0:T(8,128)(2,1)}, u32[]{:S(2)}) copy-start(bf16[2,2,1024,1024]{3,2,1,0:T(8,128)(2,1)} %param.4) | copy-start | bytes 25165828
  35.0 40.0 %copy-start.1 = (f32[64]{0:T(128)S(1)}, f32[64]{0:T(128)}, u32[]{:S(2)}) copy-start(f32[64]{0:T(128)} %param.7) | copy-start | bytes 772
  35.0 40.0 %copy-start.2 = (f32[2]{0:T(128)S(1)}, f32[2]{0:T(128)}, u32[]{:S(2)}) copy-start(f32[2]{0:T(128)} %param.6) | copy-start | bytes 28
Sparse Core Ops, SparseCore 0:
  36.3 37.7 reduce-scatter.1
where the time goes:
time: 88.6 us; the launch traced here: 88.4 us
  waiting for transfers between devices  38 us (43%)
  blocking collectives  17.6 us (20%)
  matrix products  14.8 us (17%)
  between operations  13.5 us (15%)
  local copies, waits for them, and re-layouts  3.43 us (4%)
  other arithmetic  1.16 us (1%)
    reduce_scatter x1, waiting for transfers between devices, per_device(): lax.psum_scatter(jnp.moveaxis(complex_rows(all_green, currents), 2, 0), '...  38 us
    all_gather x1, blocking collectives, per_device(): all_green = lax.all_gather(green, 'tx', axis=2, tiled=True)  17.6 us
    dot_general x2, matrix products, complex_rows(): jnp.dot(green_real, curr_imag, preferred_element_type=jnp.float32)  4.73 us
    dot_general x2, matrix products, complex_rows(): jnp.dot(green_imag, curr_imag, preferred_element_type=jnp.float32)  4.14 us
    sub x1, local copies, waits for them, and re-layouts, per_device(): gated - jnp.einsum('qc,ncm->qnm', sine_weight, receiver_portions[:, 1], p...  2.54 us
    dot_general x1, matrix products, per_device(): jnp.einsum('qc,ncm->qnm', sine_weight, receiver_portions[:, 1], precision...  2.02 us
    dot_general x1, matrix products, per_device(): jnp.einsum('qc,ncm->qnm', cosine_weight, receiver_portions[:, 0], precisi...  1.96 us
  transfers between devices with their start and end apart: 1, of which 1 were waited for; matrix products, arithmetic and copies ran while one was open for 0% of the time, Pallas kernels for 0%

commit v1 on v0

--- a/solution.py
+++ b/solution.py
@@ -27,7 +27,22 @@
     gate_phase = gate_time[:, None] * angular_freq[None, :]
     cosine_weight = jnp.cos(gate_phase)
     sine_weight = jnp.sin(gate_phase)
-    all_green = lax.all_gather(green, "tx", axis=2, tiled=True)
+    ways, here, step = (lax.axis_size("tx"), lax.axis_index("tx"), green.shape[2])
+    shape = [n * ways if d == 2 else n for d, n in enumerate(green.shape)]
+    all_green = lax.dynamic_update_slice_in_dim(
+        jnp.zeros(shape, green.dtype), green, here * step, axis=2
+    )
+    going_up = going_down = green
+    for far in range(1, ways // 2 + 1):
+        going_up = lax.ppermute(going_up, "tx", [(d, (d + 1) % ways) for d in range(ways)])
+        all_green = lax.dynamic_update_slice_in_dim(
+            all_green, going_up, (here - far) % ways * step, axis=2
+        )
+        if 2 * far < ways:
+            going_down = lax.ppermute(going_down, "tx", [(d, (d - 1) % ways) for d in range(ways)])
+            all_green = lax.dynamic_update_slice_in_dim(
+                all_green, going_down, (here + far) % ways * step, axis=2
+            )
     receiver_portions = lax.psum_scatter(
         jnp.moveaxis(complex_rows(all_green, currents), 2, 0),
         "cell",

time: 88.6 us -> 82.9 us (0.936)
  blocking collectives: 17.6 us -> 0 us
  waiting for transfers between devices: 38 us -> 45.8 us
  starting transfers between devices: 0.01 us -> 5.06 us
  matrix products: 14.8 us -> 12.6 us
  local copies, waits for them, and re-layouts: 3.43 us -> 4.45 us
    all_gather x1 -> x0, blocking collectives: 17.6 us -> none  [per_device(): all_green = lax.all_gather(green, 'tx', axis=2, tiled=True)]
    ppermute x0 -> x3, waiting for transfers between devices: none -> 10.2 us  [the longest x2 8.83 us: per_device(): lax.ppermute(going_up, 'tx', [(d, (d + 1) % ways) for d in range(ways)])]
    ppermute x0 -> x3, starting transfers between devices: none -> 5.05 us  [the longest x2 3.03 us: per_device(): lax.ppermute(going_up, 'tx', [(d, (d + 1) % ways) for d in range(ways)])]
    dot_general x2, matrix products: 4.73 us -> 0.96 us  [complex_rows(): jnp.dot(green_real, curr_imag, preferred_element_type=jnp.float32)]
    dot_general x2, matrix products: 0.96 us -> 4.14 us  [complex_rows(): jnp.dot(green_imag, curr_real, preferred_element_type=jnp.float32)]
    reduce_scatter x1, waiting for transfers between devices: 38 us -> 35.5 us  [per_device(): lax.psum_scatter(jnp.moveaxis(complex_rows(all_green, currents), 2, 0), '...]
    dot_general x2, matrix products: 4.14 us -> 2.55 us  [complex_rows(): jnp.dot(green_imag, curr_imag, preferred_element_type=jnp.float32)]
    dynamic_update_slice x0 -> x4, local copies, waits for them, and re-layouts: none -> 0.96 us  [the longest x1 0.93 us: per_device(): lax.dynamic_update_slice_in_dim(jnp.zeros(shape, green.dtype), green, her...]
  transfers between devices with their start and end apart: 1 -> 4, of which waited for: 1 -> 4; matrix products, arithmetic and copies ran while one was open for 0% -> 1% of each run, Pallas kernels for 0% -> 0%
where the time goes in v1:
time: 82.9 us; the launch traced here: 82.6 us
  waiting for transfers between devices  45.8 us (55%)
  between operations  13.6 us (16%)
  matrix products  12.6 us (15%)
  starting transfers between devices  5.06 us (6%)
  local copies, waits for them, and re-layouts  4.45 us (5%)
  other arithmetic  1.16 us (1%)
    reduce_scatter x1, waiting for transfers between devices, per_device(): lax.psum_scatter(jnp.moveaxis(complex_rows(all_green, currents), 2, 0), '...  35.5 us
    ppermute x2, waiting for transfers between devices, per_device(): lax.ppermute(going_up, 'tx', [(d, (d + 1) % ways) for d in range(ways)])  8.83 us
    dot_general x2, matrix products, complex_rows(): jnp.dot(green_imag, curr_real, preferred_element_type=jnp.float32)  4.14 us
    ppermute x2, starting transfers between devices, per_device(): lax.ppermute(going_up, 'tx', [(d, (d + 1) % ways) for d in range(ways)])  3.03 us
    dot_general x2, matrix products, complex_rows(): jnp.dot(green_imag, curr_imag, preferred_element_type=jnp.float32)  2.55 us
    sub x1, local copies, waits for them, and re-layouts, per_device(): gated - jnp.einsum('qc,ncm->qnm', sine_weight, receiver_portions[:, 1], p...  2.54 us
    ppermute x1, starting transfers between devices, per_device(): lax.ppermute(going_down, 'tx', [(d, (d - 1) % ways) for d in range(ways)])  2.03 us
    dot_general x1, matrix products, per_device(): jnp.einsum('qc,ncm->qnm', sine_weight, receiver_portions[:, 1], precision...  2.03 us
  transfers between devices with their start and end apart: 4, of which 4 were waited for; matrix products, arithmetic and copies ran while one was open for 1% of the time, Pallas kernels for 0%

profile of v1, /device:TPU:0, one launch (start us, length us, event | category | flops | bytes accessed | tf_op | source)
XLA Modules:
  0.0 82.6 jit_solution(12294898182432922167)
XLA Ops:
  6.5 0.0 reduce-scatter.2.cloned.1.call-start
  6.5 3.0 %collective-permute-start = (bf16[2,2,16,1024]{3,2,1,0:T(8,128)(2,1)}, bf16[2,2,16,1024]{3,2,1,0:T(8,128)(2,1)S(1)}, u32[]{:S(2)}, u32[]{:S(2)}) collective-permute-start(bf16[2,2,16,1024]{3,2,1,0:T(8,128)(2,1)} %param.5), channel_id=1, source_target_pairs={{0,8},{8,16},{16,24},{24,0},{1,9},{9,17},{17,25},{25,1},{2,10},{10... | collective-permute-start | bytes 393224 | tf_op jit(solution)/shard_map/ppermute | solution.py:37
  9.6 2.0 %collective-permute-start.1 = (bf16[2,2,16,1024]{3,2,1,0:T(8,128)(2,1)}, bf16[2,2,16,1024]{3,2,1,0:T(8,128)(2,1)S(1)}, u32[]{:S(2)}, u32[]{:S(2)}) collective-permute-start(bf16[2,2,16,1024]{3,2,1,0:T(8,128)(2,1)} %param.5), channel_id=1, source_target_pairs={{0,24},{8,0},{16,8},{24,16},{1,25},{9,1},{17,9},{25,17},{2,26},{10... | collective-permute-start | bytes 393224 | tf_op jit(solution)/shard_map/ppermute | solution.py:42
  11.6 0.1 broadcast_in_dim.2
  11.6 0.9 %constant_dynamic-update-slice_fusion.3 = bf16[2,2,64,1024]{3,2,1,0:T(8,128)(2,1)S(1)} fusion(bf16[2,2,64,1024]{3,2,1,0:T(8,128)(2,1)S(1)} %broadcast_in_dim.2, bf16[2,2,16,1024]{3,2,1,0:T(8,128)(2,1)} %param.5, s32[]{:T(128)S(6)} %select_n.27), kind=kLoop, calls=%fused_computation.52 | loop fusion | bytes 262148 | tf_op jit(solution)/shard_map/dynamic_update_slice | solution.py:32
  12.6 3.5 %collective-permute-done = bf16[2,2,16,1024]{3,2,1,0:T(8,128)(2,1)S(1)} collective-permute-done((bf16[2,2,16,1024]{3,2,1,0:T(8,128)(2,1)}, bf16[2,2,16,1024]{3,2,1,0:T(8,128)(2,1)S(1)}, u32[]{:S(2)}, u32[]{:S(2)}) %collective-permute-start) | collective-permute-done | bytes 131104 | tf_op jit(solution)/shard_map/ppermute | solution.py:37
  16.1 0.0 collective-permute-start.2
  16.1 0.0 copy-start
  16.2 1.4 %collective-permute-done.1 = bf16[2,2,16,1024]{3,2,1,0:T(8,128)(2,1)S(1)} collective-permute-done((bf16[2,2,16,1024]{3,2,1,0:T(8,128)(2,1)}, bf16[2,2,16,1024]{3,2,1,0:T(8,128)(2,1)S(1)}, u32[]{:S(2)}, u32[]{:S(2)}) %collective-permute-start.1) | collective-permute-done | bytes 131104 | tf_op jit(solution)/shard_map/ppermute | solution.py:42
  17.6 5.3 %collective-permute-done.2 = bf16[2,2,16,1024]{3,2,1,0:T(8,128)(2,1)S(1)} collective-permute-done((bf16[2,2,16,1024]{3,2,1,0:T(8,128)(2,1)S(1)}, bf16[2,2,16,1024]{3,2,1,0:T(8,128)(2,1)S(1)}, u32[]{:S(2)}, u32[]{:S(2)}) %collective-permute-start.2) | collective-permute-done | bytes 131104 | tf_op jit(solution)/shard_map/ppermute | solution.py:37
  22.9 2.1 %fusion.4 = f32[64,1024]{1,0:T(8,128)S(1)} fusion(bf16[2,2,1024,1024]{3,2,1,0:T(8,128)(2,1)} %param.4, bf16[2,2,64,1024]{3,2,1,0:T(8,128)(2,1)S(1)} %constant_dynamic-update-slice_fusion), kind=kOutput, calls=%fused_computation.4 | convolution fusion | flops 134217728 | bytes 2490368 | tf_op jit(solution)/shard_map/dot_general | solution.py:21
  25.0 2.1 %fusion.12 = f32[64,1024]{1,0:T(8,128)S(1)} fusion(bf16[2,2,1024,1024]{3,2,1,0:T(8,128)(2,1)} %param.4, bf16[2,2,64,1024]{3,2,1,0:T(8,128)(2,1)S(1)} %constant_dynamic-update-slice_fusion), kind=kOutput, calls=%fused_computation.12 | convolution fusion | flops 134217728 | bytes 2490368 | tf_op jit(solution)/shard_map/dot_general | solution.py:21
  27.1 2.1 %fusion.2 = f32[64,1024]{1,0:T(8,128)S(1)} fusion(bf16[2,2,1024,1024]{3,2,1,0:T(8,128)(2,1)} %param.4, bf16[2,2,64,1024]{3,2,1,0:T(8,128)(2,1)S(1)} %constant_dynamic-update-slice_fusion), kind=kOutput, calls=%fused_computation.2 | convolution fusion | flops 134217728 | bytes 2490368 | tf_op jit(solution)/shard_map/dot_general | solution.py:17
  29.1 0.0 copy-done
  29.2 0.5 fusion.10
  29.6 0.5 fusion.45
  30.1 0.5 fusion.33
  30.6 0.5 fusion.39
  31.1 0.5 fusion.27
  31.6 0.1 maximum_bitcast_fusion.1
  31.7 0.0 copy-start.1
  31.7 0.0 copy-start.2
  31.7 1.1 %maximum_bitcast_fusion = f32[64,2,2,1024]{3,0,2,1:T(8,128)} fusion(f32[1,2,64,1024]{3,2,1,0:T(8,128)S(1)} %get-tuple-element.8, f32[1,2,64,1024]{3,2,1,0:T(8,128)S(1)} %get-tuple-element.7), kind=kLoop, calls=%fused_computation.33 | loop fusion | flops 262144 | bytes 2097152 | tf_op jit(solution)/shard_map/transpose | solution.py:47
  32.8 0.0 reduce-scatter.2.cloned.1.call-update
  32.8 35.5 %reduce-scatter.2.cloned.1.call-done = f32[8,2,2,1024]{3,0,2,1:T(8,128)} async-done(((f32[64,2,2,1024]{3,0,2,1:T(8,128)}), f32[8,2,2,1024]{3,0,2,1:T(8,128)}) %reduce-scatter.2.cloned.1.call-update) | async-done | bytes 131088 | tf_op jit(solution)/shard_map/reduce_scatter | solution.py:46
  68.3 0.9 %slice_bitcast_fusion.12 = (f32[8,2,1024]{2,0,1:T(8,128)S(1)}, f32[8,2,1024]{2,0,1:T(8,128)S(1)}) fusion(f32[8,2,2,1024]{3,0,2,1:T(8,128)} %reduce-scatter.2.cloned.1.call-done), kind=kLoop, calls=%fused_computation.40 | loop fusion | bytes 262144 | tf_op jit(solution)/shard_map/squeeze | solution.py:56
  69.2 0.0 copy-done.1
  69.2 0.0 copy-done.2
  69.2 2.0 %fusion.49 = f32[64,8,1024]{2,0,1:T(8,128)S(1)} fusion(f32[8,2,1024]{2,0,1:T(8,128)S(1)} %get-tuple-element.6, f32[64]{0:T(128)S(1)} %copy-done.1, f32[2]{0:T(128)S(1)} %copy-done.2), kind=kOutput, calls=%fused_computation.43 | convolution fusion | flops 12583040 | bytes 2162952 | tf_op jit(solution)/shard_map/qc,ncm->qnm/dot_general | solution.py:52
  71.2 2.0 %convolution_subtract_fusion = f32[64,8,1024]{2,0,1:T(8,128)S(1)} fusion(f32[64,8,1024]{2,0,1:T(8,128)S(1)} %fusion.49, f32[8,2,1024]{2,0,1:T(8,128)S(1)} %get-tuple-element.5, f32[64]{0:T(128)S(1)} %copy-done.1, f32[2]{0:T(128)S(1)} %copy-done.2), kind=kOutput, calls=%fused_computation.24 | convolution fusion | flops 13107328 | bytes 4260104 | tf_op jit(solution)/shard_map/qc,ncm->qnm/dot_general | solution.py:55
  73.3 2.5 %copy.7 = f32[64,8,1024]{2,1,0:T(8,128)} copy(f32[64,8,1024]{2,0,1:T(8,128)S(1)} %convolution_subtract_fusion) | data formatting | bytes 4194304 | tf_op jit(solution)/shard_map/sub | solution.py:55
  (3 shorter events, 0.0 us)
Async XLA Ops:
  6.5 61.8 %reduce-scatter.2.cloned.1.call-start = ((), (), s32[]{:S(2)}) async-start(), calls=%async_computation.1 | async-start | bytes 1179648 | tf_op jit(solution)/shard_map/reduce_scatter | solution.py:46
  6.5 9.6 %collective-permute-start = (bf16[2,2,16,1024]{3,2,1,0:T(8,128)(2,1)}, bf16[2,2,16,1024]{3,2,1,0:T(8,128)(2,1)S(1)}, u32[]{:S(2)}, u32[]{:S(2)}) collective-permute-start(bf16[2,2,16,1024]{3,2,1,0:T(8,128)(2,1)} %param.5), channel_id=1, source_target_pairs={{0,8},{8,16},{16,24},{24,0},{1,9},{9,17},{17,25},{25,1},{2,10},{10... | collective-permute-start | bytes 393224 | tf_op jit(solution)/shard_map/ppermute | solution.py:37
  9.6 8.0 %collective-permute-start.1 = (bf16[2,2,16,1024]{3,2,1,0:T(8,128)(2,1)}, bf16[2,2,16,1024]{3,2,1,0:T(8,128)(2,1)S(1)}, u32[]{:S(2)}, u32[]{:S(2)}) collective-permute-start(bf16[2,2,16,1024]{3,2,1,0:T(8,128)(2,1)} %param.5), channel_id=1, source_target_pairs={{0,24},{8,0},{16,8},{24,16},{1,25},{9,1},{17,9},{25,17},{2,26},{10... | collective-permute-start | bytes 393224 | tf_op jit(solution)/shard_map/ppermute | solution.py:42
  16.1 6.8 %collective-permute-start.2 = (bf16[2,2,16,1024]{3,2,1,0:T(8,128)(2,1)S(1)}, bf16[2,2,16,1024]{3,2,1,0:T(8,128)(2,1)S(1)}, u32[]{:S(2)}, u32[]{:S(2)}) collective-permute-start(bf16[2,2,16,1024]{3,2,1,0:T(8,128)(2,1)S(1)} %collective-permute-done), channel_id=1, source_target_pairs={{0,8},{8,16},{16,24},{24,0},{1,9},{9,17},{17,25},{25,1},{2,10},{10... | collective-permute-start | bytes 393224 | tf_op jit(solution)/shard_map/ppermute | solution.py:37
  16.1 13.0 %copy-start = (bf16[2,2,1024,1024]{3,2,1,0:T(8,128)(2,1)S(1)}, bf16[2,2,1024,1024]{3,2,1,0:T(8,128)(2,1)}, u32[]{:S(2)}) copy-start(bf16[2,2,1024,1024]{3,2,1,0:T(8,128)(2,1)} %param.4) | copy-start | bytes 25165828
  31.7 37.6 %copy-start.1 = (f32[64]{0:T(128)S(1)}, f32[64]{0:T(128)}, u32[]{:S(2)}) copy-start(f32[64]{0:T(128)} %param.7) | copy-start | bytes 772
  31.7 37.6 %copy-start.2 = (f32[2]{0:T(128)S(1)}, f32[2]{0:T(128)}, u32[]{:S(2)}) copy-start(f32[2]{0:T(128)} %param.6) | copy-start | bytes 28
Sparse Core Ops, SparseCore 0:
  32.9 35.3 reduce-scatter.1
